TPU v7x, 32 devices: a whole 2x2x4 slice. The times are simulated.
32 devices in a mesh: dp: 8 (over y, x, core), tensor: 4 (over z).
Axes of the slice: x: 2, y: 2, z: 4, core: 2. Of those that a mesh axis runs over, the one named last changes fastest.
Arguments:
- acts: bfloat16 [3072, 4096], P('dp', 'tensor'), may hold values from -6 to 6
- grad_out: bfloat16 [3072, 4096], P('dp', 'tensor'), may hold values from -60 to 60
- gate_pre: bfloat16 [3072, 14336], P('dp', 'tensor'), may hold values from -6 to 6
- up_pre: bfloat16 [3072, 14336], P('dp', 'tensor'), may hold values from -6 to 6
- down_weight: bfloat16 [14336, 4096], P('tensor', 'dp'), may hold values from -0.09375 to 0.09375
- proj_in: bfloat16 [4096, 64], P('tensor'), may hold values from -0.09375 to 0.09375
- proj_out: bfloat16 [14336, 64], P('tensor'), may hold values from -0.046875 to 0.046875
- lengths: int32 [24], P('dp'), may hold values from 64 to 128
- query_ids: int32 [16], replicated, may hold values from 0 to 23
Outputs:
- gram: float32 [4096, 4096], P('dp', 'tensor')
- scores: float32 [16, 24], P(None, 'dp')
Inputs may be any that keep to these rules, and one draw needn't show every extreme that they name: `query_ids`: queries may repeat.
All inputs are finite; a program needn't handle non-finite values.
Results may differ from a plain program's by a relative error of at most 0.004.
Values may be sent and summed in bfloat16 or wider, within the bound.
A program may use at most 128 MiB of HBM per device.

v0:
```python
import jax
import jax.numpy as jnp
from jax import lax
from jax.sharding import PartitionSpec as P


def silu_slope(value):
    sigma = jax.nn.sigmoid(value)
    return sigma + value * sigma * (1.0 - sigma)


def body(acts, grad_out, gate_pre, up_pre, down_weight, proj_in, proj_out, lengths, query_ids):
    highest = lax.Precision.HIGHEST
    tokens_here = acts.shape[0]
    examples_here = lengths.shape[0]
    seq_len = tokens_here // examples_here
    full_grad = lax.all_gather(grad_out, "tensor", axis=1, tiled=True)
    hidden_grad = lax.dot_general(
        full_grad,
        lax.all_gather(down_weight, "dp", axis=1, tiled=True),
        (((1,), (1,)), ((), ())),
        preferred_element_type=jnp.float32,
    )
    gate_value = gate_pre.astype(jnp.float32)
    gate_grad = (hidden_grad * up_pre.astype(jnp.float32) * silu_slope(gate_value)).astype(
        jnp.bfloat16
    )
    out_part = jnp.dot(gate_grad, proj_out, preferred_element_type=jnp.float32)
    in_part = jnp.dot(acts, proj_in, preferred_element_type=jnp.float32)
    out_factor, in_factor = lax.psum((out_part, in_part), "tensor")
    positions = lax.broadcasted_iota(jnp.int32, (examples_here, seq_len), 1)
    live = (positions < lengths[:, None]).astype(jnp.float32)
    out_factor = out_factor.reshape(examples_here, seq_len, -1) * live[:, :, None]
    in_factor = in_factor.reshape(examples_here, seq_len, -1)
    features = jnp.einsum("esa,esb->eab", out_factor, in_factor, precision=highest).reshape(
        examples_here, -1
    )
    width = features.shape[1]
    first_example = lax.axis_index("dp") * examples_here
    example_ids = first_example + lax.broadcasted_iota(jnp.int32, (1, examples_here), 1)
    selector = (query_ids[:, None] == example_ids).astype(jnp.float32)
    query_part = jnp.dot(selector, features, precision=highest)
    local_square = jnp.sum(features * features)
    query_feat, total_square = lax.psum((query_part, local_square), "dp")
    examples_all = examples_here * lax.axis_size("dp")
    norm_mean = total_square / examples_all + 1e-06
    col_width = width // lax.axis_size("tensor")
    own_cols = lax.dynamic_slice_in_dim(
        features, lax.axis_index("tensor") * col_width, col_width, 1
    )
    row_block = lax.all_to_all(features, "dp", split_axis=1, concat_axis=0, tiled=True)
    block = lax.dot_general(
        row_block,
        lax.all_gather(own_cols, "dp", axis=0, tiled=True),
        (((0,), (0,)), ((), ())),
        precision=highest,
        preferred_element_type=jnp.float32,
    )
    gram = block * (width / examples_all) / norm_mean
    scores = jnp.dot(query_feat, features.T, precision=highest) / norm_mean
    return (gram, scores)


def solution(mesh):
    in_specs = (
        P("dp", "tensor"),
        P("dp", "tensor"),
        P("dp", "tensor"),
        P("dp", "tensor"),
        P("tensor", "dp"),
        P("tensor", None),
        P("tensor", None),
        P("dp"),
        P(),
    )
    out_specs = (P("dp", "tensor"), P(None, "dp"))
    return jax.shard_map(body, mesh=mesh, in_specs=in_specs, out_specs=out_specs, check_vma=False)
```

profile of v0, /device:TPU:0, one launch (start us, length us, event | category | flops | bytes accessed | tf_op | source)
XLA Modules:
  0.0 374.6 jit_solution(14562197754892564738)
XLA Ops:
  7.2 0.0 copy-start
  7.2 0.0 all-gather.4.cloned.1.call-start
  7.2 0.7 all-gather.4.cloned.1.call-update
  7.9 0.0 all-gather.6.cloned.1.call-start
  8.0 0.7 all-gather.6.cloned.1.call-update
  8.7 0.0 all-reduce.6.cloned.1.call-start
  8.8 0.4 convolution_bitcast_fusion
  9.1 0.6 copy.25
  9.8 66.0 %all-gather.4.cloned.1.call-done = bf16[384,4096]{1,0:T(8,128)(2,1)} async-done(((bf16[384,1024]{1,0:T(8,128)(2,1)}), bf16[384,4096]{1,0:T(8,128)(2,1)}) %all-gather.4.cloned.1.call-update) | async-done | bytes 3145744 | tf_op jit(solution)/shard_map/all_gather | solution.py:17
  75.8 149.3 %all-gather.6.cloned.1.call-done = bf16[3584,4096]{1,0:T(8,128)(2,1)} async-done(((bf16[3584,512]{1,0:T(8,128)(2,1)}), bf16[3584,4096]{1,0:T(8,128)(2,1)}) %all-gather.6.cloned.1.call-update) | async-done | bytes 29360144 | tf_op jit(solution)/shard_map/all_gather | solution.py:20
  225.1 0.0 copy-done.4
  225.1 20.3 %fusion.9 = f32[384,64]{0,1:T(8,128)S(1)} fusion(bf16[3584,64]{0,1:T(8,128)(2,1)S(1)} %copy-done.4, bf16[384,4096]{1,0:T(8,128)(2,1)} %all-gather.4.cloned.1.call-done, bf16[3584,4096]{1,0:T(8,128)(2,1)} %all-gather.6.cloned.1.call-done, bf16[384,3584]{1,0:T(8,128)(2,1)} %param.11, bf16[384,3584]{1,0:T(8,128)(2,1)} %param.12), kind=kOutput, calls=%fused_computation.17 | convolution fusion | flops 11466964992 | bytes 38567936 | tf_op jit(solution)/shard_map/dot_general | solution.py:28
  245.4 0.7 reshape.43
  246.1 0.0 all-reduce.6.cloned.1.call-update
  246.2 0.1 fusion.14
  246.2 35.4 %all-reduce.6.cloned.1.call-done = (f32[3,128,64]{1,2,0:T(8,128)}, f32[3,128,64]{1,0,2:T(4,128)}) async-done(((f32[3,128,64]{1,2,0:T(8,128)}, f32[3,128,64]{1,0,2:T(4,128)}), (f32[3,128,64]{1,2,0:T(8,128)}, f32[3,128,64]{1,0,2:T(4,128)})) %all-reduce.6.cloned.1.call-update) | async-done | bytes 196624 | tf_op jit(solution)/shard_map/psum | solution.py:30
  281.6 0.9 broadcast_multiply_fusion
  282.5 1.8 multiply_reduce_fusion
  284.3 0.1 all_to_all.14
  284.4 0.1 reshape.45
  284.5 0.7 copy.18
  285.2 3.6 all-to-all-start
  288.8 0.0 all-reduce.4.cloned.1.call-start
  288.8 1.0 fusion.10
  289.9 15.0 %psum.30 = f32[]{:T(128)} all-reduce(f32[]{:T(128)} %get-tuple-element.4), channel_id=1, replica_groups=mesh['dp'=8,'tensor'=4] {'dp'}, use_global_device_ids=true, to_apply=%region_3.0 | all-reduce | flops 1 | bytes 8 | tf_op jit(solution)/shard_map/psum | solution.py:44
  304.9 8.2 %all-gather = f32[8,3,1024]{2,1,0:T(4,128)S(1)} all-gather(f32[1,3,1024]{2,1,0:T(4,128)S(1)} %dynamic-slice_bitcast_fusion), channel_id=1, replica_groups=mesh['dp'=8,'tensor'=4] {'dp'}, dimensions={0}, use_global_device_ids=true | all-gather | bytes 110592 | tf_op jit(solution)/shard_map/all_gather | solution.py:54
  313.1 0.1 reshape.47
  313.2 0.0 all-reduce.4.cloned.1.call-update
  313.8 0.0 all-to-all-done
  313.9 3.2 multiply_divide_fusion
  317.1 49.0 %all-reduce.4.cloned.1.call-done = f32[16,4096]{1,0:T(8,128)} async-done(((f32[16,4096]{1,0:T(8,128)}), f32[16,4096]{1,0:T(8,128)}) %all-reduce.4.cloned.1.call-update) | async-done | bytes 262160 | tf_op jit(solution)/shard_map/psum | solution.py:44
  366.1 2.0 convolution_divide_fusion
  (11 shorter events, 0.0 us)
Async XLA Ops:
  7.2 1.6 copy-start
  7.2 1.6 copy-start.1
  7.2 217.9 %copy-start.4 = (bf16[3584,64]{0,1:T(8,128)(2,1)S(1)}, bf16[3584,64]{0,1:T(8,128)(2,1)}, u32[]{:S(2)}) copy-start(bf16[3584,64]{0,1:T(8,128)(2,1)} %param.15) | copy-start | bytes 1376260
  7.2 68.6 %all-gather.4.cloned.1.call-start = ((), (), s32[]{:S(2)}) async-start(), calls=%async_computation.1 | async-start | bytes 3932160 | tf_op jit(solution)/shard_map/all_gather | solution.py:17
  7.9 217.1 %all-gather.6.cloned.1.call-start = ((), (), s32[]{:S(2)}) async-start(), calls=%async_computation.2 | async-start | bytes 33030144 | tf_op jit(solution)/shard_map/all_gather | solution.py:20
  8.7 272.9 %all-reduce.6.cloned.1.call-start = ((), (), s32[]{:S(2)}) async-start(), calls=%async_computation.4 | async-start | bytes 458752 | tf_op jit(solution)/shard_map/psum | solution.py:30
  9.8 236.4 %copy-start.3 = (s32[3]{0:T(128)S(1)}, s32[3]{0:T(128)}, u32[]{:S(2)}) copy-start(s32[3]{0:T(128)} %param.16) | copy-start | bytes 40
  9.8 279.1 %copy-start.2 = (s32[16]{0:T(128)S(1)}, s32[16]{0:T(128)}, u32[]{:S(2)}) copy-start(s32[16]{0:T(128)} %param.17) | copy-start | bytes 196
  285.2 28.7 %all-to-all-start = ((f32[3,8,512]{2,0,1:T(4,128)}), f32[3,8,512]{2,0,1:T(4,128)S(1)}, u32[]{:S(2)}, u32[]{:S(2)}) async-start(f32[3,8,512]{2,0,1:T(4,128)} %copy.18), calls=%async_computation | async-start | bytes 131072 | tf_op jit(solution)/shard_map/all_to_all | solution.py:51
  288.8 77.3 %all-reduce.4.cloned.1.call-start = ((), (), s32[]{:S(2)}) async-start(), calls=%async_computation.3 | async-start | bytes 524288 | tf_op jit(solution)/shard_map/psum | solution.py:44
Sparse Core Ops, SparseCore 0:
  9.6 66.1 all-gather.3
  77.6 147.3 all-gather.5
  246.3 35.2 all-reduce.5
  313.3 52.7 all-reduce.3
where the time goes:
time: 375 us
  waiting for transfers between devices  301 us (80%)
  matrix products  28.7 us (8%)
  blocking collectives  23.2 us (6%)
  between operations  14.5 us (4%)
  starting transfers between devices  3.75 us (1%)
    all_gather x1, waiting for transfers between devices, body(): lax.all_gather(down_weight, 'dp', axis=1, tiled=True)  149 us
    all_gather x1, waiting for transfers between devices, body(): full_grad = lax.all_gather(grad_out, 'tensor', axis=1, tiled=True)  66 us
    psum x1, waiting for transfers between devices, body(): query_feat, total_square = lax.psum((query_part, local_square), 'dp')  49 us
    psum x1, waiting for transfers between devices, body(): out_factor, in_factor = lax.psum((out_part, in_part), 'tensor')  35.4 us
    dot_general x1, matrix products, body(): out_part = jnp.dot(gate_grad, proj_out, preferred_element_type=jnp.float32)  20.3 us
    psum x1, blocking collectives, body(): query_feat, total_square = lax.psum((query_part, local_square), 'dp')  15 us
    all_gather x1, blocking collectives, body(): lax.all_gather(own_cols, 'dp', axis=0, tiled=True)  8.25 us
  transfers between devices with their start and end apart: 5, of which 4 were waited for; matrix products, arithmetic and copies ran while one was open for 1% of the time, Pallas kernels for 0%

commit v1 on v0

--- a/solution.py
+++ b/solution.py
@@ -2,6 +2,23 @@
 import jax.numpy as jnp
 from jax import lax
 from jax.sharding import PartitionSpec as P
+from jax.lax import axis_index, axis_size, ppermute
+
+
+def set_core(field, array_dim):
+    degree = axis_size("tensor")
+    table = [(ix, (ix + 1) % degree) for ix in range(degree)]
+
+    def map_halves(current_arr):
+        if len(current_arr) == degree:
+            return current_arr
+        response = ppermute(current_arr[0], axis_name="tensor", perm=table)
+        return map_halves([response, *current_arr])
+
+    h_now = map_halves([field])
+    mid_arr = jnp.concatenate(h_now, axis=array_dim)
+    plain = axis_index("tensor")
+    return jnp.roll(mid_arr, shift=(plain + 1) * field.shape[array_dim], axis=array_dim)
 
 
 def silu_slope(value):
@@ -14,7 +31,7 @@
     tokens_here = acts.shape[0]
     examples_here = lengths.shape[0]
     seq_len = tokens_here // examples_here
-    full_grad = lax.all_gather(grad_out, "tensor", axis=1, tiled=True)
+    full_grad = set_core(grad_out, 1)
     hidden_grad = lax.dot_general(
         full_grad,
         lax.all_gather(down_weight, "dp", axis=1, tiled=True),

time: 375 us -> 285 us (0.76)
  waiting for transfers between devices: 301 us -> 196 us
  local copies, waits for them, and re-layouts: 2.3 us -> 13 us
    all_gather x1, waiting for transfers between devices: 149 us -> 79.6 us  [body(): lax.all_gather(down_weight, 'dp', axis=1, tiled=True)]
    all_gather x1 -> x0, waiting for transfers between devices: 66 us -> none  [body(): full_grad = lax.all_gather(grad_out, 'tensor', axis=1, tiled=True)]
    ppermute x0 -> x3, waiting for transfers between devices: none -> 58.1 us  [map_halves(): response = ppermute(current_arr[0], axis_name='tensor', perm=table)]
    psum x1, waiting for transfers between devices: 49 us -> 22.3 us  [body(): query_feat, total_square = lax.psum((query_part, local_square), 'dp')]
    unnamed x12 -> x17, local copies, waits for them, and re-layouts: 0.08 us -> 9.73 us
  transfers between devices with their start and end apart: 5 -> 7, of which waited for: 4 -> 6; matrix products, arithmetic and copies ran while one was open for 1% -> 6% of each run, Pallas kernels for 0% -> 0%
where the time goes in v1:
time: 285 us; the launch traced here: 284 us
  waiting for transfers between devices  196 us (69%)
  matrix products  29.6 us (10%)
  blocking collectives  23.3 us (8%)
  between operations  14.5 us (5%)
  local copies, waits for them, and re-layouts  13 us (5%)
  starting transfers between devices  6.83 us (2%)
    all_gather x1, waiting for transfers between devices, body(): lax.all_gather(down_weight, 'dp', axis=1, tiled=True)  79.6 us
    ppermute x3, waiting for transfers between devices, map_halves(): response = ppermute(current_arr[0], axis_name='tensor', perm=table)  58.1 us
    psum x1, waiting for transfers between devices, body(): out_factor, in_factor = lax.psum((out_part, in_part), 'tensor')  35.3 us
    psum x1, waiting for transfers between devices, body(): query_feat, total_square = lax.psum((query_part, local_square), 'dp')  22.3 us
    dot_general x1, matrix products, body(): out_part = jnp.dot(gate_grad, proj_out, preferred_element_type=jnp.float32)  20.4 us
    psum x1, blocking collectives, body(): query_feat, total_square = lax.psum((query_part, local_square), 'dp')  15.1 us
    unnamed x17, local copies, waits for them, and re-layouts  9.73 us
    all_gather x1, blocking collectives, body(): lax.all_gather(own_cols, 'dp', axis=0, tiled=True)  8.26 us
  transfers between devices with their start and end apart: 7, of which 6 were waited for; matrix products, arithmetic and copies ran while one was open for 6% of the time, Pallas kernels for 0%

profile of v1, /device:TPU:0, one launch (start us, length us, event | category | flops | bytes accessed | tf_op | source)
XLA Modules:
  0.0 284.2 jit_solution(3515044689885996386)
XLA Ops:
  7.2 0.7 all-gather.3.cloned.1.call-update
  8.0 3.1 %collective-permute-start = (bf16[384,1024]{1,0:T(8,128)(2,1)}, bf16[384,1024]{1,0:T(8,128)(2,1)S(1)}, u32[]{:S(2)}, u32[]{:S(2)}) collective-permute-start(bf16[384,1024]{1,0:T(8,128)(2,1)} %param.10), channel_id=1, source_target_pairs={{0,1},{1,2},{2,3},{3,0},{4,5},{5,6},{6,7},{7,4},{8,9},{9,10},{10,1... | collective-permute-start | bytes 2359304 | tf_op jit(solution)/shard_map/ppermute | solution.py:15
  11.1 19.8 %collective-permute-done = bf16[384,1024]{1,0:T(8,128)(2,1)S(1)} collective-permute-done((bf16[384,1024]{1,0:T(8,128)(2,1)}, bf16[384,1024]{1,0:T(8,128)(2,1)S(1)}, u32[]{:S(2)}, u32[]{:S(2)}) %collective-permute-start) | collective-permute-done | bytes 786464 | tf_op jit(solution)/shard_map/ppermute | solution.py:15
  30.9 20.5 %collective-permute-done.1 = bf16[384,1024]{1,0:T(8,128)(2,1)S(1)} collective-permute-done((bf16[384,1024]{1,0:T(8,128)(2,1)S(1)}, bf16[384,1024]{1,0:T(8,128)(2,1)S(1)}, u32[]{:S(2)}, u32[]{:S(2)}) %collective-permute-start.1) | collective-permute-done | bytes 786464 | tf_op jit(solution)/shard_map/ppermute | solution.py:15
  51.4 1.3 convolution_bitcast_fusion
  52.6 0.6 copy.25
  53.3 17.8 %collective-permute-done.2 = bf16[384,1024]{1,0:T(8,128)(2,1)} collective-permute-done((bf16[384,1024]{1,0:T(8,128)(2,1)S(1)}, bf16[384,1024]{1,0:T(8,128)(2,1)}, u32[]{:S(2)}, u32[]{:S(2)}) %collective-permute-start.2) | collective-permute-done | bytes 786464 | tf_op jit(solution)/shard_map/ppermute | solution.py:15
  71.1 2.4 constant_dynamic-update-slice_fusion.7
  73.5 1.0 constant_dynamic-update-slice_fusion.6
  74.5 1.0 constant_dynamic-update-slice_fusion.5
  75.5 1.0 constant_dynamic-update-slice_fusion.4
  76.5 2.2 constant_dynamic-update-slice_fusion.3
  78.7 1.0 constant_dynamic-update-slice_fusion.2
  79.7 1.0 constant_dynamic-update-slice_fusion.1
  80.8 1.0 constant_dynamic-update-slice_fusion
  81.8 79.6 %all-gather.3.cloned.1.call-done = bf16[3584,4096]{1,0:T(8,128)(2,1)} async-done(((bf16[3584,512]{1,0:T(8,128)(2,1)}), bf16[3584,4096]{1,0:T(8,128)(2,1)}) %all-gather.3.cloned.1.call-update) | async-done | bytes 29360144 | tf_op jit(solution)/shard_map/all_gather | solution.py:37
  161.4 20.4 %fusion.17 = f32[384,64]{0,1:T(8,128)S(1)} fusion(bf16[3584,64]{0,1:T(8,128)(2,1)} %param.15, bf16[3584,4096]{1,0:T(8,128)(2,1)} %all-gather.3.cloned.1.call-done, bf16[384,3584]{1,0:T(8,128)(2,1)} %param.11, bf16[384,3584]{1,0:T(8,128)(2,1)} %param.12, bf16[384,8192]{1,0:T(8,128)(2,1)} %constant_dynamic-update-slice_fusion, s32[]{:T(128)S(6)} %select_n.17), kind=kOutput, calls=%fused_computation.36 | convolution fusion | flops 11466964992 | bytes 38567940 | tf_op jit(solution)/shard_map/dot_general | solution.py:45
  181.8 0.7 reshape.43
  182.6 0.1 fusion.14
  182.6 35.3 %all-reduce.6.cloned.1.call-done = (f32[3,128,64]{1,2,0:T(8,128)}, f32[3,128,64]{1,0,2:T(4,128)}) async-done(((f32[3,128,64]{1,2,0:T(8,128)}, f32[3,128,64]{1,0,2:T(4,128)}), (f32[3,128,64]{1,2,0:T(8,128)}, f32[3,128,64]{1,0,2:T(4,128)})) %all-reduce.6.cloned.1.call-update) | async-done | bytes 196624 | tf_op jit(solution)/shard_map/psum | solution.py:47
  217.9 0.9 broadcast_multiply_fusion
  218.9 1.8 multiply_reduce_fusion
  220.7 0.1 reshape.45
  220.8 0.1 all_to_all.14
  220.9 1.0 fusion.10
  221.9 0.7 copy.18
  222.6 3.6 %all-to-all-start = ((f32[3,8,512]{2,0,1:T(4,128)}), f32[3,8,512]{2,0,1:T(4,128)S(1)}, u32[]{:S(2)}, u32[]{:S(2)}) async-start(f32[3,8,512]{2,0,1:T(4,128)} %copy.18), calls=%async_computation | async-start | bytes 131072 | tf_op jit(solution)/shard_map/all_to_all | solution.py:68
  226.2 15.1 %psum.30 = f32[]{:T(128)} all-reduce(f32[]{:T(128)} %get-tuple-element.4), channel_id=1, replica_groups=mesh['dp'=8,'tensor'=4] {'dp'}, use_global_device_ids=true, to_apply=%region_3.4 | all-reduce | flops 1 | bytes 8 | tf_op jit(solution)/shard_map/psum | solution.py:61
  241.2 8.3 %all-gather = f32[8,3,1024]{2,1,0:T(4,128)S(1)} all-gather(f32[1,3,1024]{2,1,0:T(4,128)S(1)} %dynamic-slice_bitcast_fusion), channel_id=1, replica_groups=mesh['dp'=8,'tensor'=4] {'dp'}, dimensions={0}, use_global_device_ids=true | all-gather | bytes 110592 | tf_op jit(solution)/shard_map/all_gather | solution.py:71
  250.2 3.2 %multiply_divide_fusion = f32[512,1024]{1,0:T(8,128)} fusion(f32[24,512]{1,0:T(8,128)S(1)} %all_to_all.17, f32[24,1024]{1,0:T(8,128)S(1)} %reshape.47, f32[]{:T(128)S(6)} %add.50), kind=kOutput, calls=%fused_computation.11 | convolution fusion | flops 152043520 | bytes 2244612 | tf_op jit(solution)/shard_map/dot_general | solution.py:69
  253.4 22.3 %all-reduce.4.cloned.1.call-done = f32[16,4096]{1,0:T(8,128)} async-done(((f32[16,4096]{1,0:T(8,128)}), f32[16,4096]{1,0:T(8,128)}) %all-reduce.4.cloned.1.call-update) | async-done | bytes 262160 | tf_op jit(solution)/shard_map/psum | solution.py:61
  275.8 2.0 convolution_divide_fusion
  (20 shorter events, 0.3 us)
Async XLA Ops:
  7.2 44.2 %copy-start = (bf16[384,1024]{1,0:T(8,128)(2,1)S(1)}, bf16[384,1024]{1,0:T(8,128)(2,1)}, u32[]{:S(2)}) copy-start(bf16[384,1024]{1,0:T(8,128)(2,1)} %param.9) | copy-start | bytes 2359300
  7.2 68.3 %copy-start.1 = (bf16[384,1024]{1,0:T(8,128)(2,1)S(1)}, bf16[384,1024]{1,0:T(8,128)(2,1)}, u32[]{:S(2)}) copy-start(bf16[384,1024]{1,0:T(8,128)(2,1)} %param.10) | copy-start | bytes 2359300
  7.2 154.2 %all-gather.3.cloned.1.call-start = ((), (), s32[]{:S(2)}) async-start(), calls=%async_computation.1 | async-start | bytes 33030144 | tf_op jit(solution)/shard_map/all_gather | solution.py:37
  7.9 210.0 %all-reduce.6.cloned.1.call-start = ((), (), s32[]{:S(2)}) async-start(), calls=%async_computation.3 | async-start | bytes 458752 | tf_op jit(solution)/shard_map/psum | solution.py:47
  8.0 22.9 %collective-permute-start = (bf16[384,1024]{1,0:T(8,128)(2,1)}, bf16[384,1024]{1,0:T(8,128)(2,1)S(1)}, u32[]{:S(2)}, u32[]{:S(2)}) collective-permute-start(bf16[384,1024]{1,0:T(8,128)(2,1)} %param.10), channel_id=1, source_target_pairs={{0,1},{1,2},{2,3},{3,0},{4,5},{5,6},{6,7},{7,4},{8,9},{9,10},{10,1... | collective-permute-start | bytes 2359304 | tf_op jit(solution)/shard_map/ppermute | solution.py:15
  30.9 20.5 %collective-permute-start.1 = (bf16[384,1024]{1,0:T(8,128)(2,1)S(1)}, bf16[384,1024]{1,0:T(8,128)(2,1)S(1)}, u32[]{:S(2)}, u32[]{:S(2)}) collective-permute-start(bf16[384,1024]{1,0:T(8,128)(2,1)S(1)} %collective-permute-done), channel_id=1, source_target_pairs={{0,1},{1,2},{2,3},{3,0},{4,5},{5,6},{6,7},{7,4},{8,9},{9,10},{10,1... | collective-permute-start | bytes 2359304 | tf_op jit(solution)/shard_map/ppermute | solution.py:15
  51.4 19.8 %collective-permute-start.2 = (bf16[384,1024]{1,0:T(8,128)(2,1)S(1)}, bf16[384,1024]{1,0:T(8,128)(2,1)}, u32[]{:S(2)}, u32[]{:S(2)}) collective-permute-start(bf16[384,1024]{1,0:T(8,128)(2,1)S(1)} %collective-permute-done.1), channel_id=1, source_target_pairs={{0,1},{1,2},{2,3},{3,0},{4,5},{5,6},{6,7},{7,4},{8,9},{9,10},{10,1... | collective-permute-start | bytes 2359304 | tf_op jit(solution)/shard_map/ppermute | solution.py:15
  81.8 100.8 %copy-start.3 = (s32[3]{0:T(128)S(1)}, s32[3]{0:T(128)}, u32[]{:S(2)}) copy-start(s32[3]{0:T(128)} %param.16) | copy-start | bytes 40
  81.8 139.0 %copy-start.2 = (s32[16]{0:T(128)S(1)}, s32[16]{0:T(128)}, u32[]{:S(2)}) copy-start(s32[16]{0:T(128)} %param.17) | copy-start | bytes 196
  182.5 93.3 %all-reduce.4.cloned.1.call-start = ((), (), s32[]{:S(2)}) async-start(), calls=%async_computation.2 | async-start | bytes 524288 | tf_op jit(solution)/shard_map/psum | solution.py:61
  222.6 27.6 %all-to-all-start = ((f32[3,8,512]{2,0,1:T(4,128)}), f32[3,8,512]{2,0,1:T(4,128)S(1)}, u32[]{:S(2)}, u32[]{:S(2)}) async-start(f32[3,8,512]{2,0,1:T(4,128)} %copy.18), calls=%async_computation | async-start | bytes 131072 | tf_op jit(solution)/shard_map/all_to_all | solution.py:68
Sparse Core Ops, SparseCore 0:
  9.9 151.4 all-gather.2
  182.6 35.2 all-reduce.5
  222.0 53.6 all-reduce.3
